TPU v7x, 32 devices: a whole 2x2x4 slice. The times are simulated.
32 devices in a mesh: row: 8 (over z, y), col: 4 (over x, core).
Axes of the slice: x: 2, y: 2, z: 4, core: 2. Of those that a mesh axis runs over, the one named last changes fastest.
Arguments:
- left_blocks: bfloat16 [2, 128, 512, 128], P(None, 'row', 'col'), may hold values from -0.1875 to 0.1875
- right_blocks: bfloat16 [128, 512, 128], P('row', 'col'), may hold values from -6 to 6
- left_index: int32 [2, 512, 32], P(None, 'row', 'col'), may hold values from 0 to 16, as said below
- right_index: int32 [2, 512, 32], P(None, 'row', 'col'), may hold values from 0 to 15
Outputs:
- out_blocks: bfloat16 [512, 512, 128], P('row', 'col')
Inputs may be any that keep to these rules, and one draw needn't show every extreme that they name: `left_index`: the value 16 marks a padded pair that adds nothing; in every step and on every device each result block has 1 to 8 live pairs.
All inputs are finite; a program needn't handle non-finite values.
Results may differ from a plain program's by a relative error of at most 0.001.
Values may be sent and summed in bfloat16 or wider, within the bound.
No kernel may reach another device: no remote copies, remote signals or barrier semaphores. Data moves between devices by JAX's collectives and lax.ppermute only.
A program may use at most 128 MiB of HBM per device.

v0:
```python
import jax
import jax.numpy as jnp
from jax import lax
from jax.sharding import PartitionSpec as P


def from_root(value, axis, source):
    kept = jnp.where(lax.axis_index(axis) == source, value, 0).astype(value.dtype)
    return lax.psum(kept, axis)


def shifted(x, axis, by):
    size = lax.axis_size(axis)
    return lax.ppermute(x, axis, [(i, (i + by) % size) for i in range(size)])


def fetch_left(left_blocks, step_index, row_at, row_count, col_count):
    panel_index = (row_at + step_index) % row_count
    own_slot = panel_index // col_count
    root_col = panel_index % col_count
    own_panel = lax.dynamic_index_in_dim(left_blocks, own_slot, 0, keepdims=False)
    fetched = from_root(own_panel, "col", root_col)
    return fetched


def grouped(left_panel, right_panel, left_rows, right_rows):
    block_size = left_panel.shape[-1]
    padded = jnp.concatenate(
        [left_panel, jnp.zeros((1, block_size, block_size), left_panel.dtype)], axis=0
    )
    slot_count, group_size = left_rows.shape
    bundle_size = min(slot_count, 32)

    def one_bundle(indices):
        left_tiles = jnp.take(padded, indices[0], axis=0)
        right_tiles = jnp.take(right_panel, indices[1], axis=0)
        return jnp.einsum(
            "sgij,sgjl->sil", left_tiles, right_tiles, preferred_element_type=jnp.float32
        )

    bundled = (
        left_rows.reshape(slot_count // bundle_size, bundle_size, group_size),
        right_rows.reshape(slot_count // bundle_size, bundle_size, group_size),
    )
    result = lax.map(one_bundle, bundled)
    return result.reshape(slot_count, block_size, block_size)


def per_device(left_blocks, right_blocks, left_index, right_index):
    row_count = lax.axis_size("row")
    col_count = lax.axis_size("col")
    row_at = lax.axis_index("row")
    step_count = left_index.shape[0]
    accumulated = None
    right_panel = right_blocks
    for step_index in range(step_count):
        if step_index > 0:
            right_panel = shifted(right_panel, "row", -1)
        left_panel = fetch_left(left_blocks, step_index, row_at, row_count, col_count)
        contribution = grouped(
            left_panel, right_panel, left_index[step_index], right_index[step_index]
        )
        accumulated = contribution if accumulated is None else accumulated + contribution
    return accumulated.astype(jnp.bfloat16)


def solution(mesh):
    return jax.shard_map(
        per_device,
        mesh=mesh,
        in_specs=(
            P(None, "row", "col", None),
            P("row", "col", None),
            P(None, "row", "col"),
            P(None, "row", "col"),
        ),
        out_specs=P("row", "col", None),
        check_vma=False,
    )
```

profile of v0, /device:TPU:0, one launch (start us, length us, event | category | flops | bytes accessed | tf_op | source)
XLA Modules:
  0.0 170.9 jit_solution(15086971149026818629)
XLA Ops:
  6.5 0.0 all-reduce.5.cloned.1.call-start
  6.5 2.2 %select_bitcast_fusion = (bf16[16,128,128]{2,1,0:T(8,128)(2,1)}, bf16[16,128,128]{2,1,0:T(8,128)(2,1)}) fusion(bf16[2,16,128,128]{3,2,1,0:T(8,128)(2,1)} %param.12, s32[]{:T(128)S(6)} %select_n.77, pred[]{:T(512)S(6)} %eq.12, s32[]{:T(128)S(6)} %select_n.70, pred[]{:T(512)S(6)} %eq.11), kind=kLoop, calls=%fused_computation.33 | loop fusion | flops 524288 | bytes 2097162 | tf_op jit(solution)/shard_map/jit(_where)/select_n | solution.py:8
  8.8 0.0 all-reduce.5.cloned.1.call-update
  8.8 6.1 %collective-permute-start = (bf16[16,128,128]{2,1,0:T(8,128)(2,1)}, bf16[16,128,128]{2,1,0:T(8,128)(2,1)S(1)}, u32[]{:S(2)}, u32[]{:S(2)}) collective-permute-start(bf16[16,128,128]{2,1,0:T(8,128)(2,1)} %param.13), channel_id=1, source_target_pairs={{0,28},{4,0},{8,4},{12,8},{16,12},{20,16},{24,20},{28,24},{1,29},{... | collective-permute-start | bytes 1572872 | tf_op jit(solution)/shard_map/ppermute | solution.py:14
  14.9 0.7 fusion.23
  15.6 0.1 copy.11
  15.7 0.7 fusion.22
  16.4 0.1 copy.12
  16.5 0.1 copy.9
  16.6 0.1 copy.10
  16.6 32.1 %all-reduce.5.cloned.1.call-done = (bf16[16,128,128]{2,1,0:T(8,128)(2,1)}, bf16[16,128,128]{2,1,0:T(8,128)(2,1)}) async-done(((bf16[16,128,128]{2,1,0:T(8,128)(2,1)}, bf16[16,128,128]{2,1,0:T(8,128)(2,1)}), (bf16[16,128,128]{2,1,0:T(8,128)(2,1)}, bf16[16,128,128]{2,1,0:T(8,128)(2,1)})) %all-reduce.5.cloned.1.call-update) | async-done | bytes 1048592 | tf_op jit(solution)/shard_map/psum | solution.py:9
  48.8 1.1 concatenate.7
  49.9 0.0 collective-permute-done
  49.9 2.5 %broadcast.27.clone.1 = f32[2,32,128,128]{3,2,1,0:T(8,128)} broadcast(f32[]{:T(128)} %constant.99.clone.1), dimensions={} | broadcast | bytes 4194308 | tf_op jit(solution)/shard_map/broadcast.2
  52.3 0.0 copy-start.1
  52.3 0.0 copy-start
  52.3 51.7 %while.21 = (s32[]{:T(128)}, f32[2,32,128,128]{3,2,1,0:T(8,128)}, s32[2,32,8]{2,1,0:T(8,128)S(1)}, bf16[17,128,128]{2,1,0:T(8,128)(2,1)S(1)}, s32[2,32,8]{2,1,0:...) while((s32[]{:T(128)}, f32[2,32,128,128]{3,2,1,0:T(8,128)}, s32[2,32,8]{2,1,0:T(8,128)S(1)}, ...), condition=%wide.region_5.8_spmd, body=%wide.region_4.7_spmd.sunk | while | flops 1082135552 | bytes 52450896 | solution.py:45
  52.4 0.1 reshape.100
  52.5 8.6 %gather_fusion.2 = bf16[256,128,128]{2,1,0:T(8,128)(2,1)} fusion(bf16[16,128,128]{2,1,0:T(8,128)(2,1)S(1)} %get-tuple-element.247, s32[1024]{0:T(1024)S(1)} %pad_clamp_fusion.10), kind=kCustom, calls=%fused_computation.3.clone.clone.1 | custom fusion | bytes 16778240 | tf_op jit(solution)/shard_map/while/body/eval_jaxpr/jit(_take)/gather | solution.py:36
  61.0 0.1 reshape.101
  61.1 8.5 %gather_fusion.3 = bf16[256,128,128]{2,1,0:T(8,128)(2,1)} fusion(bf16[17,128,128]{2,1,0:T(8,128)(2,1)S(1)} %get-tuple-element.245, s32[1024]{0:T(1024)S(1)} %pad_clamp_fusion.11), kind=kCustom, calls=%fused_computation.2.clone.clone.1 | custom fusion | bytes 16778240 | tf_op jit(solution)/shard_map/while/body/eval_jaxpr/jit(_take)/gather | solution.py:35
  69.6 8.6 %bitcast_dynamic-update-slice_fusion.5 = f32[2,32,128,128]{3,2,1,0:T(8,128)} fusion(f32[2,32,128,128]{3,2,1,0:T(8,128)} %get-tuple-element.236, s32[]{:T(128)} %get-tuple-element.235, bf16[32,8,128,128]{3,2,1,0:T(8,128)(2,1)} %bitcast.45, pred[32,8]{1,0:T(8,128)(4,1)S(1)} %get-tuple-element.204, bf16[32,8,128,128]{3,2,1,0:T(8,128)(2,1)} %bitcast.47, ...), kind=kOutput, calls=%fused_computation.24.clone.1 | convolution fusion | flops 1082130432 | bytes 18875392 | tf_op jit(solution)/shard_map/while/body/eval_jaxpr/sgij,sgjl->sil/dot_general | solution.py:37
  78.2 0.1 reshape.100
  78.3 8.6 %gather_fusion.2 = bf16[256,128,128]{2,1,0:T(8,128)(2,1)} fusion(bf16[16,128,128]{2,1,0:T(8,128)(2,1)S(1)} %get-tuple-element.247, s32[1024]{0:T(1024)S(1)} %pad_clamp_fusion.10), kind=kCustom, calls=%fused_computation.3.clone.clone.1 | custom fusion | bytes 16778240 | tf_op jit(solution)/shard_map/while/body/eval_jaxpr/jit(_take)/gather | solution.py:36
  86.9 0.1 reshape.101
  87.0 8.5 %gather_fusion.3 = bf16[256,128,128]{2,1,0:T(8,128)(2,1)} fusion(bf16[17,128,128]{2,1,0:T(8,128)(2,1)S(1)} %get-tuple-element.245, s32[1024]{0:T(1024)S(1)} %pad_clamp_fusion.11), kind=kCustom, calls=%fused_computation.2.clone.clone.1 | custom fusion | bytes 16778240 | tf_op jit(solution)/shard_map/while/body/eval_jaxpr/jit(_take)/gather | solution.py:35
  95.5 8.6 %bitcast_dynamic-update-slice_fusion.5 = f32[2,32,128,128]{3,2,1,0:T(8,128)} fusion(f32[2,32,128,128]{3,2,1,0:T(8,128)} %get-tuple-element.236, s32[]{:T(128)} %get-tuple-element.235, bf16[32,8,128,128]{3,2,1,0:T(8,128)(2,1)} %bitcast.45, pred[32,8]{1,0:T(8,128)(4,1)S(1)} %get-tuple-element.204, bf16[32,8,128,128]{3,2,1,0:T(8,128)(2,1)} %bitcast.47, ...), kind=kOutput, calls=%fused_computation.24.clone.1 | convolution fusion | flops 1082130432 | bytes 18875392 | tf_op jit(solution)/shard_map/while/body/eval_jaxpr/sgij,sgjl->sil/dot_general | solution.py:37
  104.0 0.0 copy-done.1
  104.1 2.5 %broadcast.27.clone = f32[2,32,128,128]{3,2,1,0:T(8,128)} broadcast(f32[]{:T(128)} %constant.99.clone.1), dimensions={} | broadcast | bytes 4194308 | tf_op jit(solution)/shard_map/broadcast.2
  106.6 0.0 copy-done
  106.6 51.8 %while.20 = (s32[]{:T(128)}, f32[2,32,128,128]{3,2,1,0:T(8,128)}, s32[2,32,8]{2,1,0:T(8,128)S(1)}, bf16[17,128,128]{2,1,0:T(8,128)(2,1)S(1)}, s32[2,32,8]{2,1,0:...) while((s32[]{:T(128)}, f32[2,32,128,128]{3,2,1,0:T(8,128)}, s32[2,32,8]{2,1,0:T(8,128)S(1)}, ...), condition=%wide.region_2.5_spmd, body=%wide.region_1.4_spmd.sunk | while | flops 1082135552 | bytes 52450896 | solution.py:45
  106.6 0.1 reshape.94
  106.7 8.6 %gather_fusion = bf16[256,128,128]{2,1,0:T(8,128)(2,1)} fusion(bf16[16,128,128]{2,1,0:T(8,128)(2,1)S(1)} %get-tuple-element.226, s32[1024]{0:T(1024)S(1)} %pad_clamp_fusion.8), kind=kCustom, calls=%fused_computation.1.clone.clone.1 | custom fusion | bytes 16778240 | tf_op jit(solution)/shard_map/while/body/eval_jaxpr/jit(_take)/gather | solution.py:36
  115.3 0.1 reshape.95
  115.4 8.5 %gather_fusion.1 = bf16[256,128,128]{2,1,0:T(8,128)(2,1)} fusion(bf16[17,128,128]{2,1,0:T(8,128)(2,1)S(1)} %get-tuple-element.224, s32[1024]{0:T(1024)S(1)} %pad_clamp_fusion.9), kind=kCustom, calls=%fused_computation.clone.clone.1 | custom fusion | bytes 16778240 | tf_op jit(solution)/shard_map/while/body/eval_jaxpr/jit(_take)/gather | solution.py:35
  123.9 8.6 %bitcast_dynamic-update-slice_fusion.4 = f32[2,32,128,128]{3,2,1,0:T(8,128)} fusion(f32[2,32,128,128]{3,2,1,0:T(8,128)} %get-tuple-element.215, s32[]{:T(128)} %get-tuple-element.214, bf16[32,8,128,128]{3,2,1,0:T(8,128)(2,1)} %bitcast.46, pred[32,8]{1,0:T(8,128)(4,1)S(1)} %get-tuple-element.194, bf16[32,8,128,128]{3,2,1,0:T(8,128)(2,1)} %bitcast.48, ...), kind=kOutput, calls=%fused_computation.10.clone.1 | convolution fusion | flops 1082130432 | bytes 18875392 | tf_op jit(solution)/shard_map/while/body/eval_jaxpr/sgij,sgjl->sil/dot_general | solution.py:37
  132.4 0.1 reshape.94
  132.5 8.6 %gather_fusion = bf16[256,128,128]{2,1,0:T(8,128)(2,1)} fusion(bf16[16,128,128]{2,1,0:T(8,128)(2,1)S(1)} %get-tuple-element.226, s32[1024]{0:T(1024)S(1)} %pad_clamp_fusion.8), kind=kCustom, calls=%fused_computation.1.clone.clone.1 | custom fusion | bytes 16778240 | tf_op jit(solution)/shard_map/while/body/eval_jaxpr/jit(_take)/gather | solution.py:36
  141.1 0.1 reshape.95
  141.2 8.5 %gather_fusion.1 = bf16[256,128,128]{2,1,0:T(8,128)(2,1)} fusion(bf16[17,128,128]{2,1,0:T(8,128)(2,1)S(1)} %get-tuple-element.224, s32[1024]{0:T(1024)S(1)} %pad_clamp_fusion.9), kind=kCustom, calls=%fused_computation.clone.clone.1 | custom fusion | bytes 16778240 | tf_op jit(solution)/shard_map/while/body/eval_jaxpr/jit(_take)/gather | solution.py:35
  149.8 8.5 %bitcast_dynamic-update-slice_fusion.4 = f32[2,32,128,128]{3,2,1,0:T(8,128)} fusion(f32[2,32,128,128]{3,2,1,0:T(8,128)} %get-tuple-element.215, s32[]{:T(128)} %get-tuple-element.214, bf16[32,8,128,128]{3,2,1,0:T(8,128)(2,1)} %bitcast.46, pred[32,8]{1,0:T(8,128)(4,1)S(1)} %get-tuple-element.194, bf16[32,8,128,128]{3,2,1,0:T(8,128)(2,1)} %bitcast.48, ...), kind=kOutput, calls=%fused_computation.10.clone.1 | convolution fusion | flops 1082130432 | bytes 18875392 | tf_op jit(solution)/shard_map/while/body/eval_jaxpr/sgij,sgjl->sil/dot_general | solution.py:37
  158.3 5.7 %add_convert_fusion = bf16[2,32,128,128]{3,2,1,0:T(8,128)(2,1)} fusion(f32[2,32,128,128]{3,2,1,0:T(8,128)} %get-tuple-element.71, f32[2,32,128,128]{3,2,1,0:T(8,128)} %get-tuple-element.72), kind=kLoop, calls=%fused_computation.32 | loop fusion | flops 2097152 | bytes 10485760 | tf_op jit(solution)/shard_map/convert_element_type | solution.py:64
  (13 shorter events, 0.2 us)
Async XLA Ops:
  6.5 42.2 %all-reduce.5.cloned.1.call-start = ((), (), s32[]{:S(2)}) async-start(), calls=%async_computation | async-start | bytes 2097152 | tf_op jit(solution)/shard_map/psum | solution.py:9
  8.8 41.1 %collective-permute-start = (bf16[16,128,128]{2,1,0:T(8,128)(2,1)}, bf16[16,128,128]{2,1,0:T(8,128)(2,1)S(1)}, u32[]{:S(2)}, u32[]{:S(2)}) collective-permute-start(bf16[16,128,128]{2,1,0:T(8,128)(2,1)} %param.13), channel_id=1, source_target_pairs={{0,28},{4,0},{8,4},{12,8},{16,12},{20,16},{24,20},{28,24},{1,29},{... | collective-permute-start | bytes 1572872 | tf_op jit(solution)/shard_map/ppermute | solution.py:14
  52.3 51.7 %copy-start.1 = (bf16[16,128,128]{2,1,0:T(8,128)(2,1)S(1)}, bf16[16,128,128]{2,1,0:T(8,128)(2,1)}, u32[]{:S(2)}) copy-start(bf16[16,128,128]{2,1,0:T(8,128)(2,1)} %get-tuple-element.97) | copy-start | bytes 1572868
  52.3 54.2 %copy-start = (bf16[16,128,128]{2,1,0:T(8,128)(2,1)S(1)}, bf16[16,128,128]{2,1,0:T(8,128)(2,1)}, u32[]{:S(2)}) copy-start(bf16[16,128,128]{2,1,0:T(8,128)(2,1)} %param.13) | copy-start | bytes 1572868
Sparse Core Ops, SparseCore 0:
  9.8 38.9 all-reduce.4
where the time goes:
time: 171 us
  local copies, waits for them, and re-layouts  76.8 us (45%)
  matrix products  34.2 us (20%)
  waiting for transfers between devices  32.1 us (19%)
  between operations  13.4 us (8%)
  other arithmetic  8.06 us (5%)
  starting transfers between devices  6.09 us (4%)
    gather x4, local copies, waits for them, and re-layouts, one_bundle(): right_tiles = jnp.take(right_panel, indices[1], axis=0)  34.3 us
    dot_general x4, matrix products, one_bundle(): jnp.einsum('sgij,sgjl->sil', left_tiles, right_tiles, preferred_element_t...  34.2 us
    gather x4, local copies, waits for them, and re-layouts, one_bundle(): left_tiles = jnp.take(padded, indices[0], axis=0)  34 us
    psum x1, waiting for transfers between devices, from_root(): return lax.psum(kept, axis)  32.1 us
    ppermute x1, starting transfers between devices, shifted(): return lax.ppermute(x, axis, [(i, (i + by) % size) for i in range(size)])  6.09 us
    convert_element_type x1, other arithmetic, per_device(): return accumulated.astype(jnp.bfloat16)  5.69 us
    another operation x2, local copies, waits for them, and re-layouts  4.94 us
  transfers between devices with their start and end apart: 2, of which 1 were waited for; matrix products, arithmetic and copies ran while one was open for 2% of the time, Pallas kernels for 0%

commit v1 on v0

--- a/solution.py
+++ b/solution.py
@@ -6,7 +6,7 @@
 
 def from_root(value, axis, source):
     kept = jnp.where(lax.axis_index(axis) == source, value, 0).astype(value.dtype)
-    return lax.psum(kept, axis)
+    return jnp.sum(lax.all_gather(kept, axis), axis=0)
 
 
 def shifted(x, axis, by):

time: 171 us -> 160 us (0.936)
  waiting for transfers between devices: 32.1 us -> 17.6 us
  other arithmetic: 8.06 us -> 12.1 us
    psum x1 -> x0, waiting for transfers between devices: 32.1 us -> none  [from_root(): return lax.psum(kept, axis)]
    all_gather x0 -> x2, waiting for transfers between devices: none -> 17.6 us  [from_root(): return jnp.sum(lax.all_gather(kept, axis), axis=0)]
    reduce_sum x0 -> x2, other arithmetic: none -> 4.05 us  [from_root(): return jnp.sum(lax.all_gather(kept, axis), axis=0)]
  transfers between devices with their start and end apart: 2 -> 3, of which waited for: 1 -> 1; matrix products, arithmetic and copies ran while one was open for 2% -> 36% of each run, Pallas kernels for 0% -> 0%
where the time goes in v1:
time: 160 us
  local copies, waits for them, and re-layouts  75.9 us (47%)
  matrix products  34.3 us (21%)
  waiting for transfers between devices  17.6 us (11%)
  between operations  13.4 us (8%)
  other arithmetic  12.1 us (8%)
  starting transfers between devices  6.13 us (4%)
    gather x4, local copies, waits for them, and re-layouts, one_bundle(): right_tiles = jnp.take(right_panel, indices[1], axis=0)  34.4 us
    dot_general x4, matrix products, one_bundle(): jnp.einsum('sgij,sgjl->sil', left_tiles, right_tiles, preferred_element_t...  34.3 us
    gather x4, local copies, waits for them, and re-layouts, one_bundle(): left_tiles = jnp.take(padded, indices[0], axis=0)  34 us
    all_gather x2, waiting for transfers between devices, from_root(): return jnp.sum(lax.all_gather(kept, axis), axis=0)  17.6 us
    ppermute x1, starting transfers between devices, shifted(): return lax.ppermute(x, axis, [(i, (i + by) % size) for i in range(size)])  6.09 us
    convert_element_type x1, other arithmetic, per_device(): return accumulated.astype(jnp.bfloat16)  5.69 us
    another operation x2, local copies, waits for them, and re-layouts  4.95 us
    reduce_sum x2, other arithmetic, from_root(): return jnp.sum(lax.all_gather(kept, axis), axis=0)  4.05 us
  transfers between devices with their start and end apart: 3, of which 1 were waited for; matrix products, arithmetic and copies ran while one was open for 36% of the time, Pallas kernels for 0%

profile of v1, /device:TPU:0, one launch (start us, length us, event | category | flops | bytes accessed | tf_op | source)
XLA Modules:
  0.0 159.5 jit_solution(12808851025311508207)
XLA Ops:
  6.5 0.0 all-gather.5.cloned.1.call-start
  6.5 2.2 %dynamic-slice_select_fusion = (bf16[1,16,128,128]{3,2,1,0:T(8,128)(2,1)}, bf16[1,16,128,128]{3,2,1,0:T(8,128)(2,1)}) fusion(bf16[2,16,128,128]{3,2,1,0:T(8,128)(2,1)} %param.12, s32[]{:T(128)S(6)} %select_n.72, pred[]{:T(512)S(6)} %eq.12, s32[]{:T(128)S(6)} %select_n.66, pred[]{:T(512)S(6)} %eq.11), kind=kLoop, calls=%fused_computation.33 | loop fusion | flops 524288 | bytes 2097162 | tf_op jit(solution)/shard_map/jit(_where)/select_n | solution.py:8
  8.8 0.0 all-gather.5.cloned.1.call-update
  8.8 0.0 all-gather.3.cloned.1.call-start
  8.9 6.1 %collective-permute-start = (bf16[16,128,128]{2,1,0:T(8,128)(2,1)}, bf16[16,128,128]{2,1,0:T(8,128)(2,1)S(1)}, u32[]{:S(2)}, u32[]{:S(2)}) collective-permute-start(bf16[16,128,128]{2,1,0:T(8,128)(2,1)} %param.13), channel_id=1, source_target_pairs={{0,28},{4,0},{8,4},{12,8},{16,12},{20,16},{24,20},{28,24},{1,29},{... | collective-permute-start | bytes 1572872 | tf_op jit(solution)/shard_map/ppermute | solution.py:14
  14.9 0.0 all-gather.3.cloned.1.call-update
  15.0 0.7 fusion.23
  15.7 0.1 copy.15
  15.8 0.7 fusion.22
  16.5 0.1 copy.16
  16.5 0.1 copy.13
  16.6 0.1 copy.14
  16.7 17.5 %all-gather.5.cloned.1.call-done = bf16[4,16,128,128]{3,2,1,0:T(8,128)(2,1)} async-done(((bf16[1,16,128,128]{3,2,1,0:T(8,128)(2,1)}), bf16[4,16,128,128]{3,2,1,0:T(8,128)(2,1)}) %all-gather.5.cloned.1.call-update) | async-done | bytes 2097168 | tf_op jit(solution)/shard_map/all_gather | solution.py:9
  34.3 2.0 %reduce_sum.25 = bf16[16,128,128]{2,1,0:T(8,128)(2,1)S(1)} reduce(bf16[4,16,128,128]{3,2,1,0:T(8,128)(2,1)} %all-gather.5.cloned.1.call-done, bf16[]{:T(256)} %constant.113.clone.1), dimensions={0}, to_apply=%region_3.6 | reduce | flops 786432 | bytes 2621442 | tf_op jit(solution)/shard_map/reduce_sum | solution.py:9
  36.3 0.1 concatenate.7
  36.4 0.0 collective-permute-done
  36.4 2.5 %broadcast.24.clone.1 = f32[2,32,128,128]{3,2,1,0:T(8,128)} broadcast(f32[]{:T(128)} %constant.102.clone.1), dimensions={} | broadcast | bytes 4194308 | tf_op jit(solution)/shard_map/broadcast.2
  38.9 0.0 copy-start
  38.9 51.8 %while.21 = (s32[]{:T(128)}, f32[2,32,128,128]{3,2,1,0:T(8,128)}, s32[2,32,8]{2,1,0:T(8,128)S(1)}, bf16[17,128,128]{2,1,0:T(8,128)(2,1)S(1)}, s32[2,32,8]{2,1,0:...) while((s32[]{:T(128)}, f32[2,32,128,128]{3,2,1,0:T(8,128)}, s32[2,32,8]{2,1,0:T(8,128)S(1)}, ...), condition=%wide.region_5.8_spmd, body=%wide.region_4.7_spmd.sunk | while | flops 1082135552 | bytes 52450896 | solution.py:45
  38.9 0.1 reshape.94
  39.0 8.6 %gather_fusion.2 = bf16[256,128,128]{2,1,0:T(8,128)(2,1)} fusion(bf16[16,128,128]{2,1,0:T(8,128)(2,1)S(1)} %get-tuple-element.245, s32[1024]{0:T(1024)S(1)} %pad_clamp_fusion.10), kind=kCustom, calls=%fused_computation.3.clone.clone.1 | custom fusion | bytes 16778240 | tf_op jit(solution)/shard_map/while/body/eval_jaxpr/jit(_take)/gather | solution.py:36
  47.6 0.1 reshape.95
  47.7 8.5 %gather_fusion.3 = bf16[256,128,128]{2,1,0:T(8,128)(2,1)} fusion(bf16[17,128,128]{2,1,0:T(8,128)(2,1)S(1)} %get-tuple-element.243, s32[1024]{0:T(1024)S(1)} %pad_clamp_fusion.11), kind=kCustom, calls=%fused_computation.2.clone.clone.1 | custom fusion | bytes 16778240 | tf_op jit(solution)/shard_map/while/body/eval_jaxpr/jit(_take)/gather | solution.py:35
  56.2 8.6 %bitcast_dynamic-update-slice_fusion.5 = f32[2,32,128,128]{3,2,1,0:T(8,128)} fusion(f32[2,32,128,128]{3,2,1,0:T(8,128)} %get-tuple-element.234, s32[]{:T(128)} %get-tuple-element.233, bf16[32,8,128,128]{3,2,1,0:T(8,128)(2,1)} %bitcast.41, pred[32,8]{1,0:T(8,128)(4,1)S(1)} %get-tuple-element.202, bf16[32,8,128,128]{3,2,1,0:T(8,128)(2,1)} %bitcast.43, ...), kind=kOutput, calls=%fused_computation.24.clone.1 | convolution fusion | flops 1082130432 | bytes 18875392 | tf_op jit(solution)/shard_map/while/body/eval_jaxpr/sgij,sgjl->sil/dot_general | solution.py:37
  64.8 0.1 reshape.94
  64.9 8.6 %gather_fusion.2 = bf16[256,128,128]{2,1,0:T(8,128)(2,1)} fusion(bf16[16,128,128]{2,1,0:T(8,128)(2,1)S(1)} %get-tuple-element.245, s32[1024]{0:T(1024)S(1)} %pad_clamp_fusion.10), kind=kCustom, calls=%fused_computation.3.clone.clone.1 | custom fusion | bytes 16778240 | tf_op jit(solution)/shard_map/while/body/eval_jaxpr/jit(_take)/gather | solution.py:36
  73.5 0.1 reshape.95
  73.6 8.5 %gather_fusion.3 = bf16[256,128,128]{2,1,0:T(8,128)(2,1)} fusion(bf16[17,128,128]{2,1,0:T(8,128)(2,1)S(1)} %get-tuple-element.243, s32[1024]{0:T(1024)S(1)} %pad_clamp_fusion.11), kind=kCustom, calls=%fused_computation.2.clone.clone.1 | custom fusion | bytes 16778240 | tf_op jit(solution)/shard_map/while/body/eval_jaxpr/jit(_take)/gather | solution.py:35
  82.1 8.6 %bitcast_dynamic-update-slice_fusion.5 = f32[2,32,128,128]{3,2,1,0:T(8,128)} fusion(f32[2,32,128,128]{3,2,1,0:T(8,128)} %get-tuple-element.234, s32[]{:T(128)} %get-tuple-element.233, bf16[32,8,128,128]{3,2,1,0:T(8,128)(2,1)} %bitcast.41, pred[32,8]{1,0:T(8,128)(4,1)S(1)} %get-tuple-element.202, bf16[32,8,128,128]{3,2,1,0:T(8,128)(2,1)} %bitcast.43, ...), kind=kOutput, calls=%fused_computation.24.clone.1 | convolution fusion | flops 1082130432 | bytes 18875392 | tf_op jit(solution)/shard_map/while/body/eval_jaxpr/sgij,sgjl->sil/dot_general | solution.py:37
  90.6 0.0 all-gather.3.cloned.1.call-done
  90.6 2.0 %reduce_sum.24 = bf16[16,128,128]{2,1,0:T(8,128)(2,1)S(1)} reduce(bf16[4,16,128,128]{3,2,1,0:T(8,128)(2,1)} %all-gather.3.cloned.1.call-done, bf16[]{:T(256)} %constant.113.clone.1), dimensions={0}, to_apply=%region_0.1 | reduce | flops 786432 | bytes 2621442 | tf_op jit(solution)/shard_map/reduce_sum | solution.py:9
  92.7 0.1 concatenate.6
  92.7 2.5 %broadcast.24.clone = f32[2,32,128,128]{3,2,1,0:T(8,128)} broadcast(f32[]{:T(128)} %constant.102.clone.1), dimensions={} | broadcast | bytes 4194308 | tf_op jit(solution)/shard_map/broadcast.2
  95.2 0.0 copy-done
  95.2 51.8 %while.20 = (s32[]{:T(128)}, f32[2,32,128,128]{3,2,1,0:T(8,128)}, s32[2,32,8]{2,1,0:T(8,128)S(1)}, bf16[17,128,128]{2,1,0:T(8,128)(2,1)S(1)}, s32[2,32,8]{2,1,0:...) while((s32[]{:T(128)}, f32[2,32,128,128]{3,2,1,0:T(8,128)}, s32[2,32,8]{2,1,0:T(8,128)S(1)}, ...), condition=%wide.region_2.5_spmd, body=%wide.region_1.4_spmd.sunk | while | flops 1082135552 | bytes 52450896 | solution.py:45
  95.2 0.1 reshape.88
  95.3 8.6 %gather_fusion = bf16[256,128,128]{2,1,0:T(8,128)(2,1)} fusion(bf16[16,128,128]{2,1,0:T(8,128)(2,1)S(1)} %get-tuple-element.224, s32[1024]{0:T(1024)S(1)} %pad_clamp_fusion.8), kind=kCustom, calls=%fused_computation.1.clone.clone.1 | custom fusion | bytes 16778240 | tf_op jit(solution)/shard_map/while/body/eval_jaxpr/jit(_take)/gather | solution.py:36
  103.9 0.1 reshape.89
  104.0 8.5 %gather_fusion.1 = bf16[256,128,128]{2,1,0:T(8,128)(2,1)} fusion(bf16[17,128,128]{2,1,0:T(8,128)(2,1)S(1)} %get-tuple-element.222, s32[1024]{0:T(1024)S(1)} %pad_clamp_fusion.9), kind=kCustom, calls=%fused_computation.clone.clone.1 | custom fusion | bytes 16778240 | tf_op jit(solution)/shard_map/while/body/eval_jaxpr/jit(_take)/gather | solution.py:35
  112.5 8.6 %bitcast_dynamic-update-slice_fusion.4 = f32[2,32,128,128]{3,2,1,0:T(8,128)} fusion(f32[2,32,128,128]{3,2,1,0:T(8,128)} %get-tuple-element.213, s32[]{:T(128)} %get-tuple-element.212, bf16[32,8,128,128]{3,2,1,0:T(8,128)(2,1)} %bitcast.42, pred[32,8]{1,0:T(8,128)(4,1)S(1)} %get-tuple-element.192, bf16[32,8,128,128]{3,2,1,0:T(8,128)(2,1)} %bitcast.44, ...), kind=kOutput, calls=%fused_computation.10.clone.1 | convolution fusion | flops 1082130432 | bytes 18875392 | tf_op jit(solution)/shard_map/while/body/eval_jaxpr/sgij,sgjl->sil/dot_general | solution.py:37
  121.1 0.1 reshape.88
  121.2 8.6 %gather_fusion = bf16[256,128,128]{2,1,0:T(8,128)(2,1)} fusion(bf16[16,128,128]{2,1,0:T(8,128)(2,1)S(1)} %get-tuple-element.224, s32[1024]{0:T(1024)S(1)} %pad_clamp_fusion.8), kind=kCustom, calls=%fused_computation.1.clone.clone.1 | custom fusion | bytes 16778240 | tf_op jit(solution)/shard_map/while/body/eval_jaxpr/jit(_take)/gather | solution.py:36
  129.8 0.1 reshape.89
  129.9 8.5 %gather_fusion.1 = bf16[256,128,128]{2,1,0:T(8,128)(2,1)} fusion(bf16[17,128,128]{2,1,0:T(8,128)(2,1)S(1)} %get-tuple-element.222, s32[1024]{0:T(1024)S(1)} %pad_clamp_fusion.9), kind=kCustom, calls=%fused_computation.clone.clone.1 | custom fusion | bytes 16778240 | tf_op jit(solution)/shard_map/while/body/eval_jaxpr/jit(_take)/gather | solution.py:35
  138.4 8.5 %bitcast_dynamic-update-slice_fusion.4 = f32[2,32,128,128]{3,2,1,0:T(8,128)} fusion(f32[2,32,128,128]{3,2,1,0:T(8,128)} %get-tuple-element.213, s32[]{:T(128)} %get-tuple-element.212, bf16[32,8,128,128]{3,2,1,0:T(8,128)(2,1)} %bitcast.42, pred[32,8]{1,0:T(8,128)(4,1)S(1)} %get-tuple-element.192, bf16[32,8,128,128]{3,2,1,0:T(8,128)(2,1)} %bitcast.44, ...), kind=kOutput, calls=%fused_computation.10.clone.1 | convolution fusion | flops 1082130432 | bytes 18875392 | tf_op jit(solution)/shard_map/while/body/eval_jaxpr/sgij,sgjl->sil/dot_general | solution.py:37
  147.0 5.7 %add_convert_fusion = bf16[2,32,128,128]{3,2,1,0:T(8,128)(2,1)} fusion(f32[2,32,128,128]{3,2,1,0:T(8,128)} %get-tuple-element.71, f32[2,32,128,128]{3,2,1,0:T(8,128)} %get-tuple-element.72), kind=kLoop, calls=%fused_computation.32 | loop fusion | flops 2097152 | bytes 10485760 | tf_op jit(solution)/shard_map/convert_element_type | solution.py:64
  (12 shorter events, 0.1 us)
Async XLA Ops:
  6.5 27.7 %all-gather.5.cloned.1.call-start = ((), (), s32[]{:S(2)}) async-start(), calls=%async_computation.1 | async-start | bytes 2621440 | tf_op jit(solution)/shard_map/all_gather | solution.py:9
  8.8 81.8 %all-gather.3.cloned.1.call-start = ((), (), s32[]{:S(2)}) async-start(), calls=%async_computation | async-start | bytes 2621440 | tf_op jit(solution)/shard_map/all_gather | solution.py:9
  8.9 27.5 %collective-permute-start = (bf16[16,128,128]{2,1,0:T(8,128)(2,1)}, bf16[16,128,128]{2,1,0:T(8,128)(2,1)S(1)}, u32[]{:S(2)}, u32[]{:S(2)}) collective-permute-start(bf16[16,128,128]{2,1,0:T(8,128)(2,1)} %param.13), channel_id=1, source_target_pairs={{0,28},{4,0},{8,4},{12,8},{16,12},{20,16},{24,20},{28,24},{1,29},{... | collective-permute-start | bytes 1572872 | tf_op jit(solution)/shard_map/ppermute | solution.py:14
  38.9 56.3 %copy-start = (bf16[16,128,128]{2,1,0:T(8,128)(2,1)S(1)}, bf16[16,128,128]{2,1,0:T(8,128)(2,1)}, u32[]{:S(2)}) copy-start(bf16[16,128,128]{2,1,0:T(8,128)(2,1)} %param.13) | copy-start | bytes 1572868
Sparse Core Ops, SparseCore 0:
  8.9 25.2 all-gather.4
  35.8 22.5 all-gather.2
